TPU v7x, 128 devices: a whole 4x4x4 slice. The times are simulated.
128 devices in a mesh: hi: 16 (over y, x), lo: 8 (over z, core).
Axes of the slice: x: 4, y: 4, z: 4, core: 2. Of those that a mesh axis runs over, the one named last changes fastest.
Arguments:
- previous: float32 [32, 2097152], P(None, ('hi', 'lo')), may hold values from -6 to 6
- current: float32 [32, 2097152], P(None, ('hi', 'lo')), may hold values from -6 to 6
- field_levels: int32 [21], replicated, may hold values from -4 to 4
- bond_levels: int32 [20], replicated, may hold values from 1 to 3
Outputs:
- ortho_block: float32 [32, 2097152], P(None, ('hi', 'lo'))
- upper_factor: float32 [32, 32], replicated
All inputs are finite; a program needn't handle non-finite values.
Results may differ from a plain program's by a relative error of at most 0.00005.
Values sent between devices are 32-bit elements; how exact they have to be, the bound alone decides.
A program may use at most 64 MiB of HBM per device.

v0:
```python
import jax
import jax.numpy as jnp
from jax import lax
from jax.sharding import PartitionSpec as P

FIELD_STEP = 0.75
COUPLING_STEP = 0.5


def chain_matrix(couplings, bit_count, bond_list):
    width = 2**bit_count
    rows = lax.iota(jnp.int32, width)[:, None]
    cols = lax.iota(jnp.int32, width)[None, :]
    matrix = jnp.zeros((width, width), jnp.float32)
    for site_number, spot in bond_list:
        differ = cols >> spot & 1 != cols >> spot + 1 & 1
        target = rows == cols ^ 3 << spot
        matrix = matrix + jnp.where(differ & target, 0.5 * couplings[site_number], 0.0)
    return matrix


def cross_flip(values, coupling, low_spot):
    width = values.shape[-1]
    index = lax.iota(jnp.int32, width)
    permute = (index[:, None] == index[None, :] ^ 1 << low_spot).astype(jnp.float32)
    moved = jnp.einsum("vatbl,lj->vatbj", values, permute, precision=lax.Precision.HIGHEST)
    flipped = jnp.flip(moved, axis=2)
    upper = lax.iota(jnp.int32, 2)[:, None]
    keep = (index[None, :] >> low_spot & 1 != upper).astype(jnp.float32)
    return 0.5 * coupling * flipped * keep[None, None, :, None, :]


def local(previous, current, field_levels, bond_levels):
    vectors, amp_count = current.shape
    site_count = field_levels.shape[0]
    devices = lax.axis_size("hi") * lax.axis_size("lo")
    local_bits = amp_count.bit_length() - 1
    global_bits = devices.bit_length() - 1
    rest_bits = local_bits - global_bits
    device = lax.axis_index("hi") * lax.axis_size("lo") + lax.axis_index("lo")
    local_index = lax.iota(jnp.int32, amp_count)
    top_width = 2**global_bits
    low_width = 2**rest_bits

    def position(site_number):
        if site_number < global_bits:
            return rest_bits + site_number
        return site_number - global_bits

    def spin_value(site_number):
        if site_number < local_bits:
            return 0.5 - (local_index >> position(site_number) & 1).astype(jnp.float32)
        return 0.5 - (device >> site_number - local_bits & 1).astype(jnp.float32)

    fields = FIELD_STEP * field_levels.astype(jnp.float32)
    couplings = COUPLING_STEP * bond_levels.astype(jnp.float32)
    diagonal = jnp.zeros((amp_count,), jnp.float32)
    for site_number in range(site_count):
        diagonal = diagonal + fields[site_number] * spin_value(site_number)
        if site_number < site_count - 1:
            diagonal = diagonal + couplings[site_number] * spin_value(site_number) * spin_value(
                site_number + 1
            )
    top_matrix = chain_matrix(
        couplings,
        global_bits,
        [(site_number, site_number) for site_number in range(global_bits - 1)],
    )
    low_matrix = chain_matrix(
        couplings,
        rest_bits,
        [
            (site_number, site_number - global_bits)
            for site_number in range(global_bits, local_bits - 1)
        ],
    )
    blocks = current.reshape(vectors, top_width, low_width)
    applied = diagonal[None, :] * current
    applied = applied + jnp.einsum(
        "vtl,tu->vul", blocks, top_matrix, precision=lax.Precision.HIGHEST
    ).reshape(vectors, amp_count)
    applied = applied + jnp.einsum(
        "vtl,lu->vtu", blocks, low_matrix, precision=lax.Precision.HIGHEST
    ).reshape(vectors, amp_count)
    joined = cross_flip(
        current.reshape(vectors, 1, 2, top_width // 2, low_width), couplings[global_bits - 1], 0
    )
    applied = applied + joined.reshape(vectors, amp_count)
    far_matrix = chain_matrix(
        couplings,
        global_bits,
        [
            (site_number, site_number - local_bits)
            for site_number in range(local_bits, site_count - 1)
        ],
    )
    shaped = current.reshape(vectors, devices, amp_count // devices)
    arrived = lax.all_to_all(shaped, ("hi", "lo"), split_axis=1, concat_axis=1, tiled=True)
    count = arrived.shape[0]
    bond_terms = jnp.einsum(
        "vtl,tu->vul", arrived, far_matrix, precision=lax.Precision.HIGHEST
    ).reshape(count, amp_count)
    seam = cross_flip(
        arrived.reshape(count, top_width // 2, 2, 1, low_width),
        couplings[local_bits - 1],
        rest_bits - 1,
    )
    bond_terms = bond_terms + seam.reshape(count, amp_count)
    remote_part = lax.all_to_all(
        bond_terms.reshape(arrived.shape), ("hi", "lo"), split_axis=1, concat_axis=1, tiled=True
    ).reshape(vectors, amp_count)
    filtered = 4.0 / site_count * (applied + remote_part) - previous
    local_gram = jnp.dot(filtered, filtered.T, precision=lax.Precision.HIGHEST) / (
        amp_count * devices
    )
    gram_matrix = lax.psum(local_gram, ("hi", "lo"))
    lower_factor = jnp.linalg.cholesky(gram_matrix)
    inverse = jax.scipy.linalg.solve_triangular(
        lower_factor, jnp.eye(vectors, dtype=jnp.float32), lower=True
    )
    ortho_block = jnp.dot(inverse, filtered, precision=lax.Precision.HIGHEST)
    return (ortho_block, lower_factor.T)


def solution(mesh):
    in_specs = (P(None, ("hi", "lo")), P(None, ("hi", "lo")), P(), P())
    out_specs = (P(None, ("hi", "lo")), P())
    return jax.shard_map(local, mesh=mesh, in_specs=in_specs, out_specs=out_specs, check_vma=False)
```

profile of v0, /device:TPU:1, one launch (start us, length us, event | category | flops | bytes accessed | tf_op | source)
XLA Modules:
  0.0 200.1 jit_solution(15617030087911046846)
XLA Ops:
  0.6 3.2 %copy_bitcast_fusion = f32[32,128,128]{2,0,1:T(8,128)} fusion(f32[32,16384]{1,0:T(8,128)} %param.5), kind=kLoop, calls=%fused_computation.6 | loop fusion | bytes 4194304 | tf_op jit(solution)/shard_map/reshape | solution.py:77
  3.8 11.5 %all-to-all-start = ((f32[32,128,128]{2,0,1:T(8,128)}), f32[32,128,128]{2,0,1:T(8,128)S(1)}, u32[]{:S(2)}, u32[]{:S(2)}) async-start(f32[32,128,128]{2,0,1:T(8,128)} %copy_bitcast_fusion), calls=%async_computation | async-start | bytes 4194304 | tf_op jit(solution)/shard_map/all_to_all | solution.py:98
  15.3 0.0 copy-done
  15.4 0.7 fusion.153
  20.4 25.0 %all-to-all-done = f32[32,128,128]{2,0,1:T(8,128)S(1)} async-done(((f32[32,128,128]{2,0,1:T(8,128)}), f32[32,128,128]{2,0,1:T(8,128)S(1)}, u32[]{:S(2)}, u32[]{:S(2)}) %all-to-all-start) | async-done | bytes 2097184 | tf_op jit(solution)/shard_map/all_to_all | solution.py:98
  45.4 2.3 %fusion.7 = f32[32,64,2,128]{3,1,2,0:T(8,128)S(1)} fusion(f32[32,64,2,128]{3,0,2,1:T(8,128)S(1)} %bitcast.129, s32[128]{0:T(128)S(1)} %iota_xor_fusion), kind=kOutput, calls=%fused_computation.14 | convolution fusion | flops 805322752 | bytes 4194816 | tf_op jit(solution)/shard_map/vatbl,lj->vatbj/dot_general | solution.py:26
  47.7 0.3 multiply_multiply_fusion
  48.1 1.7 copy.31
  49.8 3.2 %bitcast_add_fusion.3 = f32[32,128,128]{2,1,0:T(8,128)S(1)} fusion(f32[32,128,128]{2,1,0:T(8,128)S(1)} %bitcast.133, f32[32,128,128]{2,0,1:T(8,128)S(1)} %all-to-all-done, f32[]{:T(128)S(6)} %mul.670, f32[]{:T(128)S(6)} %mul.669, f32[]{:T(128)S(6)} %mul.668, f32[]{:T(128)S(6)} %mul.667, f32[]{:T(128)S(6)} %mul.666, f32[]{:T(128)S(6)} %mul.665, ...), kind=kOutput, calls=%fused_computation.7 | convolution fusion | flops 806207488 | bytes 6295320 | tf_op jit(solution)/shard_map/vtl,tu->vul/dot_general | solution.py:100
  53.0 2.5 %copy.32 = f32[32,128,128]{2,0,1:T(8,128)} copy(f32[32,128,128]{2,1,0:T(8,128)S(1)} %bitcast_add_fusion.3) | data formatting | bytes 4194304 | tf_op jit(solution)/shard_map/add | solution.py:108
  55.5 5.9 %all-to-all-start.1 = ((f32[32,128,128]{2,0,1:T(8,128)}), f32[32,128,128]{2,0,1:T(8,128)}, u32[]{:S(2)}, u32[]{:S(2)}) async-start(f32[32,128,128]{2,0,1:T(8,128)} %copy.32), calls=%async_computation.1 | async-start | bytes 4194304 | tf_op jit(solution)/shard_map/all_to_all | solution.py:109
  61.4 0.7 fusion.151
  74.1 2.0 copy.42
  76.1 3.4 %convolution_bitcast_fusion.1 = f32[32,128,128]{1,2,0:T(8,128)} fusion(f32[32,128,128]{2,1,0:T(8,128)S(1)} %bitcast.125, f32[]{:T(128)S(6)} %mul.659, f32[]{:T(128)S(6)} %mul.658, f32[]{:T(128)S(6)} %mul.657, f32[]{:T(128)S(6)} %mul.656, f32[]{:T(128)S(6)} %mul.655, f32[]{:T(128)S(6)} %mul.654, s32[128]{0:T(128)S(1)} %get-tuple-element.52, ...), kind=kOutput, calls=%fused_computation.16 | convolution fusion | flops 805683200 | bytes 4198168 | tf_op jit(solution)/shard_map/vtl,lu->vtu/dot_general | solution.py:82
  79.5 2.9 %copy.27 = f32[32,128,128]{2,1,0:T(8,128)} copy(f32[32,128,128]{1,2,0:T(8,128)} %convolution_bitcast_fusion.1) | data formatting | bytes 4194304 | tf_op jit(solution)/shard_map/vtl,lu->vtu/dot_general | solution.py:82
  86.2 0.6 fusion.152
  86.7 17.3 %add_add_fusion = f32[16384]{0:T(1024)S(1)} fusion(f32[]{:T(128)S(6)} %mul.645, f32[]{:T(128)S(6)} %mul.644, f32[]{:T(128)S(6)} %mul.642, f32[]{:T(128)S(6)} %mul.641, f32[]{:T(128)S(6)} %mul.639, f32[]{:T(128)S(6)} %mul.638, f32[]{:T(128)S(6)} %mul.636, f32[]{:T(128)S(6)} %mul.635, f32[]{:T(128)S(6)} %mul.633, f32[]{:T(128)S(6)} %mul.632, f32[]{:T(128)S(6)} %mul.630, ...), kind=kLoop, calls=%fused_computation.63 | loop fusion | flops 2260992 | bytes 65704 | tf_op jit(solution)/shard_map/add | solution.py:59
  104.1 1.1 convolution_bitcast_fusion
  105.2 1.6 multiply_multiply_fusion.1
  106.8 3.4 %fusion.14 = f32[128,32,128]{2,0,1:T(8,128)} fusion(f32[32,128,128]{2,1,0:T(8,128)S(1)} %bitcast.127, f32[]{:T(128)S(6)} %mul.653, s32[128]{0:T(128)S(1)} %get-tuple-element.52, f32[]{:T(128)S(6)} %mul.652, s32[128]{0:T(128)S(1)} %get-tuple-element.53, f32[]{:T(128)S(6)} %mul.651, s32[128]{0:T(128)S(1)} %get-tuple-element.54, f32[]{:T(128)S(6)} %mul.650, ...), kind=kOutput, calls=%fused_computation.20 | convolution fusion | flops 805683200 | bytes 4198168 | tf_op jit(solution)/shard_map/vtl,tu->vul/dot_general | solution.py:79
  110.2 0.0 all-to-all-done.1
  110.2 9.6 %fusion.2 = f32[32,16384]{1,0:T(8,128)S(1)} fusion(f32[32,16384]{1,0:T(8,128)} %param.4, f32[4,8,128,128]{3,2,1,0:T(8,128)} %bitcast.130, f32[4,8,128,128]{3,2,1,0:T(8,128)} %bitcast.132, f32[4,8,128,128]{3,2,1,0:T(8,128)} %bitcast.131, f32[32,16384]{1,0:T(8,128)} %param.5, f32[16384]{0:T(1024)S(1)} %add_add_fusion, f32[32,128,128]{2,0,1:T(8,128)} %all-to-all-done.1), kind=kLoop, calls=%fused_computation.3 | loop fusion | flops 3670016 | bytes 14745600 | tf_op jit(solution)/shard_map/sub | solution.py:112
  119.8 1.8 convolution_multiply_fusion
  121.6 67.6 %psum.7 = f32[32,32]{0,1:T(8,128)S(1)} all-reduce(f32[32,32]{0,1:T(8,128)S(1)} %convolution_multiply_fusion), channel_id=1, replica_groups=mesh['hi'=16,'lo'=8] {'hi','lo'}, use_global_device_ids=true, to_apply=%region_0.1 | all-reduce | flops 1024 | bytes 8192 | tf_op jit(solution)/shard_map/psum | solution.py:116
  189.2 0.1 copy.35
  189.3 2.9 %cholesky.17 = f32[32,32]{1,0:T(8,128)S(1)} custom-call(f32[32,32]{1,0:T(8,128)S(1)} %fusion.138), custom_call_target="Cholesky" | custom-call | tf_op jit(solution)/shard_map/jit(cholesky)/cholesky | solution.py:117
  192.2 0.6 compare_reduce_fusion
  192.9 0.7 fusion.139
  193.5 2.4 %custom-call.7 = f32[1,32,32]{1,2,0:T(8,128)S(1)} custom-call(f32[1,32,32]{2,1,0:T(8,128)S(1)} %get-tuple-element.11), custom_call_target="InvertDiagBlocksLowerTriangular" | custom-call | tf_op jit(solution)/shard_map/jit(_solve_triangular)/triangular_solve | solution.py:118
  196.0 0.2 fusion.136
  196.2 3.2 %fusion.154 = f32[32,16384]{1,0:T(8,128)} fusion(f32[32,32]{1,0:T(8,128)S(1)} %fusion.136, f32[32,16384]{1,0:T(8,128)S(1)} %fusion.2), kind=kOutput, calls=%fused_computation.175 | convolution fusion | flops 201326592 | bytes 4198400 | tf_op jit(solution)/shard_map/dot_general | solution.py:121
  199.4 0.7 copy.36
  (19 shorter events, 0.1 us)
Async XLA Ops:
  3.8 11.5 %copy-start = (s32[20]{0:T(128)S(1)}, s32[20]{0:T(128)}, u32[]{:S(2)}) copy-start(s32[20]{0:T(128)} %param.7) | copy-start | bytes 244
  3.8 16.6 %copy-start.1 = (s32[21]{0:T(128)S(1)}, s32[21]{0:T(128)}, u32[]{:S(2)}) copy-start(s32[21]{0:T(128)} %param.6) | copy-start | bytes 256
  3.8 41.6 %all-to-all-start = ((f32[32,128,128]{2,0,1:T(8,128)}), f32[32,128,128]{2,0,1:T(8,128)S(1)}, u32[]{:S(2)}, u32[]{:S(2)}) async-start(f32[32,128,128]{2,0,1:T(8,128)} %copy_bitcast_fusion), calls=%async_computation | async-start | bytes 4194304 | tf_op jit(solution)/shard_map/all_to_all | solution.py:98
  55.5 54.7 %all-to-all-start.1 = ((f32[32,128,128]{2,0,1:T(8,128)}), f32[32,128,128]{2,0,1:T(8,128)}, u32[]{:S(2)}, u32[]{:S(2)}) async-start(f32[32,128,128]{2,0,1:T(8,128)} %copy.32), calls=%async_computation.1 | async-start | bytes 4194304 | tf_op jit(solution)/shard_map/all_to_all | solution.py:109
where the time goes:
time: 201 us; the launch traced here: 200 us
  blocking collectives  67.6 us (34%)
  other arithmetic  35.6 us (18%)
  waiting for transfers between devices  25 us (12%)
  between operations  20.7 us (10%)
  matrix products  18.7 us (9%)
  starting transfers between devices  17.4 us (9%)
  local copies, waits for them, and re-layouts  15.1 us (8%)
    psum x1, blocking collectives, local(): gram_matrix = lax.psum(local_gram, ('hi', 'lo'))  67.6 us
    all_to_all x1, waiting for transfers between devices, local(): lax.all_to_all(shaped, ('hi', 'lo'), split_axis=1, concat_axis=1, tiled=T...  25 us
    add x1, other arithmetic, local(): diagonal = diagonal + fields[site_number] * spin_value(site_number)  17.3 us
    all_to_all x1, starting transfers between devices, local(): lax.all_to_all(shaped, ('hi', 'lo'), split_axis=1, concat_axis=1, tiled=T...  11.5 us
    sub x1, other arithmetic, local(): filtered = 4.0 / site_count * (applied + remote_part) - previous  9.63 us
    all_to_all x1, starting transfers between devices, local(): lax.all_to_all(bond_terms.reshape(arrived.shape), ('hi', 'lo'), split_axi...  5.89 us
  transfers between devices with their start and end apart: 2, of which 1 were waited for; matrix products, arithmetic and copies ran while one was open for 17% of the time, Pallas kernels for 0%

commit v1 on v0

--- a/solution.py
+++ b/solution.py
@@ -113,7 +113,7 @@
     local_gram = jnp.dot(filtered, filtered.T, precision=lax.Precision.HIGHEST) / (
         amp_count * devices
     )
-    gram_matrix = lax.psum(local_gram, ("hi", "lo"))
+    gram_matrix = lax.psum(lax.psum(local_gram, "hi"), "lo")
     lower_factor = jnp.linalg.cholesky(gram_matrix)
     inverse = jax.scipy.linalg.solve_triangular(
         lower_factor, jnp.eye(vectors, dtype=jnp.float32), lower=True

time: 201 us -> 231 us (1.15)
  blocking collectives: 67.6 us -> 95.5 us
    psum x1 -> x2, blocking collectives: 67.6 us -> 95.5 us  [local(): gram_matrix = lax.psum(lax.psum(local_gram, 'hi'), 'lo')]
  transfers between devices with their start and end apart: 2 -> 2, of which waited for: 1 -> 1; matrix products, arithmetic and copies ran while one was open for 17% -> 15% of each run, Pallas kernels for 0% -> 0%
where the time goes in v1:
time: 231 us; the launch traced here: 228 us
  blocking collectives  95.5 us (41%)
  other arithmetic  35.6 us (15%)
  waiting for transfers between devices  24.8 us (11%)
  between operations  21 us (9%)
  matrix products  18.6 us (8%)
  starting transfers between devices  17.4 us (8%)
  local copies, waits for them, and re-layouts  15.1 us (7%)
    psum x2, blocking collectives, local(): gram_matrix = lax.psum(lax.psum(local_gram, 'hi'), 'lo')  95.5 us
    all_to_all x1, waiting for transfers between devices, local(): lax.all_to_all(shaped, ('hi', 'lo'), split_axis=1, concat_axis=1, tiled=T...  24.8 us
    add x1, other arithmetic, local(): diagonal = diagonal + fields[site_number] * spin_value(site_number)  17.3 us
    all_to_all x1, starting transfers between devices, local(): lax.all_to_all(shaped, ('hi', 'lo'), split_axis=1, concat_axis=1, tiled=T...  11.5 us
    sub x1, other arithmetic, local(): filtered = 4.0 / site_count * (applied + remote_part) - previous  9.63 us
    all_to_all x1, starting transfers between devices, local(): lax.all_to_all(bond_terms.reshape(arrived.shape), ('hi', 'lo'), split_axi...  5.89 us
  transfers between devices with their start and end apart: 2, of which 1 were waited for; matrix products, arithmetic and copies ran while one was open for 15% of the time, Pallas kernels for 0%

profile of v1, /device:TPU:1, one launch (start us, length us, event | category | flops | bytes accessed | tf_op | source)
XLA Modules:
  0.0 228.0 jit_solution(5453678326594752027)
XLA Ops:
  0.6 3.2 %copy_bitcast_fusion = f32[32,128,128]{2,0,1:T(8,128)} fusion(f32[32,16384]{1,0:T(8,128)} %param.5), kind=kLoop, calls=%fused_computation.6 | loop fusion | bytes 4194304 | tf_op jit(solution)/shard_map/reshape | solution.py:77
  3.8 11.5 %all-to-all-start = ((f32[32,128,128]{2,0,1:T(8,128)}), f32[32,128,128]{2,0,1:T(8,128)S(1)}, u32[]{:S(2)}, u32[]{:S(2)}) async-start(f32[32,128,128]{2,0,1:T(8,128)} %copy_bitcast_fusion), calls=%async_computation | async-start | bytes 4194304 | tf_op jit(solution)/shard_map/all_to_all | solution.py:98
  15.4 0.7 fusion.153
  20.7 24.8 %all-to-all-done = f32[32,128,128]{2,0,1:T(8,128)S(1)} async-done(((f32[32,128,128]{2,0,1:T(8,128)}), f32[32,128,128]{2,0,1:T(8,128)S(1)}, u32[]{:S(2)}, u32[]{:S(2)}) %all-to-all-start) | async-done | bytes 2097184 | tf_op jit(solution)/shard_map/all_to_all | solution.py:98
  45.4 2.3 %fusion.7 = f32[32,64,2,128]{3,1,2,0:T(8,128)S(1)} fusion(f32[32,64,2,128]{3,0,2,1:T(8,128)S(1)} %bitcast.129, s32[128]{0:T(128)S(1)} %iota_xor_fusion), kind=kOutput, calls=%fused_computation.14 | convolution fusion | flops 805322752 | bytes 4194816 | tf_op jit(solution)/shard_map/vatbl,lj->vatbj/dot_general | solution.py:26
  47.7 0.3 multiply_multiply_fusion
  48.1 1.7 copy.31
  49.8 3.2 %bitcast_add_fusion.3 = f32[32,128,128]{2,1,0:T(8,128)S(1)} fusion(f32[32,128,128]{2,1,0:T(8,128)S(1)} %bitcast.133, f32[32,128,128]{2,0,1:T(8,128)S(1)} %all-to-all-done, f32[]{:T(128)S(6)} %mul.670, f32[]{:T(128)S(6)} %mul.669, f32[]{:T(128)S(6)} %mul.668, f32[]{:T(128)S(6)} %mul.667, f32[]{:T(128)S(6)} %mul.666, f32[]{:T(128)S(6)} %mul.665, ...), kind=kOutput, calls=%fused_computation.7 | convolution fusion | flops 806207488 | bytes 6295320 | tf_op jit(solution)/shard_map/vtl,tu->vul/dot_general | solution.py:100
  53.0 2.5 %copy.32 = f32[32,128,128]{2,0,1:T(8,128)} copy(f32[32,128,128]{2,1,0:T(8,128)S(1)} %bitcast_add_fusion.3) | data formatting | bytes 4194304 | tf_op jit(solution)/shard_map/add | solution.py:108
  55.5 5.9 %all-to-all-start.1 = ((f32[32,128,128]{2,0,1:T(8,128)}), f32[32,128,128]{2,0,1:T(8,128)}, u32[]{:S(2)}, u32[]{:S(2)}) async-start(f32[32,128,128]{2,0,1:T(8,128)} %copy.32), calls=%async_computation.1 | async-start | bytes 4194304 | tf_op jit(solution)/shard_map/all_to_all | solution.py:109
  61.4 0.7 fusion.151
  74.0 2.0 copy.42
  75.9 3.4 %convolution_bitcast_fusion.1 = f32[32,128,128]{1,2,0:T(8,128)} fusion(f32[32,128,128]{2,1,0:T(8,128)S(1)} %bitcast.125, f32[]{:T(128)S(6)} %mul.659, f32[]{:T(128)S(6)} %mul.658, f32[]{:T(128)S(6)} %mul.657, f32[]{:T(128)S(6)} %mul.656, f32[]{:T(128)S(6)} %mul.655, f32[]{:T(128)S(6)} %mul.654, s32[128]{0:T(128)S(1)} %get-tuple-element.52, ...), kind=kOutput, calls=%fused_computation.16 | convolution fusion | flops 805683200 | bytes 4198168 | tf_op jit(solution)/shard_map/vtl,lu->vtu/dot_general | solution.py:82
  79.4 2.9 %copy.27 = f32[32,128,128]{2,1,0:T(8,128)} copy(f32[32,128,128]{1,2,0:T(8,128)} %convolution_bitcast_fusion.1) | data formatting | bytes 4194304 | tf_op jit(solution)/shard_map/vtl,lu->vtu/dot_general | solution.py:82
  86.1 0.6 fusion.152
  86.7 17.3 %add_add_fusion = f32[16384]{0:T(1024)S(1)} fusion(f32[]{:T(128)S(6)} %mul.645, f32[]{:T(128)S(6)} %mul.644, f32[]{:T(128)S(6)} %mul.642, f32[]{:T(128)S(6)} %mul.641, f32[]{:T(128)S(6)} %mul.639, f32[]{:T(128)S(6)} %mul.638, f32[]{:T(128)S(6)} %mul.636, f32[]{:T(128)S(6)} %mul.635, f32[]{:T(128)S(6)} %mul.633, f32[]{:T(128)S(6)} %mul.632, f32[]{:T(128)S(6)} %mul.630, ...), kind=kLoop, calls=%fused_computation.63 | loop fusion | flops 2260992 | bytes 65704 | tf_op jit(solution)/shard_map/add | solution.py:59
  104.0 1.1 convolution_bitcast_fusion
  105.2 1.6 multiply_multiply_fusion.1
  106.7 3.4 %fusion.14 = f32[128,32,128]{2,0,1:T(8,128)} fusion(f32[32,128,128]{2,1,0:T(8,128)S(1)} %bitcast.127, f32[]{:T(128)S(6)} %mul.653, s32[128]{0:T(128)S(1)} %get-tuple-element.52, f32[]{:T(128)S(6)} %mul.652, s32[128]{0:T(128)S(1)} %get-tuple-element.53, f32[]{:T(128)S(6)} %mul.651, s32[128]{0:T(128)S(1)} %get-tuple-element.54, f32[]{:T(128)S(6)} %mul.650, ...), kind=kOutput, calls=%fused_computation.20 | convolution fusion | flops 805683200 | bytes 4198168 | tf_op jit(solution)/shard_map/vtl,tu->vul/dot_general | solution.py:79
  110.1 0.0 all-to-all-done.1
  110.1 9.6 %fusion.2 = f32[32,16384]{1,0:T(8,128)S(1)} fusion(f32[32,16384]{1,0:T(8,128)} %param.4, f32[4,8,128,128]{3,2,1,0:T(8,128)} %bitcast.130, f32[4,8,128,128]{3,2,1,0:T(8,128)} %bitcast.132, f32[4,8,128,128]{3,2,1,0:T(8,128)} %bitcast.131, f32[32,16384]{1,0:T(8,128)} %param.5, f32[16384]{0:T(1024)S(1)} %add_add_fusion, f32[32,128,128]{2,0,1:T(8,128)} %all-to-all-done.1), kind=kLoop, calls=%fused_computation.3 | loop fusion | flops 3670016 | bytes 14745600 | tf_op jit(solution)/shard_map/sub | solution.py:112
  119.8 1.8 convolution_multiply_fusion
  121.5 60.4 %psum.14 = f32[32,32]{0,1:T(8,128)S(1)} all-reduce(f32[32,32]{0,1:T(8,128)S(1)} %convolution_multiply_fusion), channel_id=1, replica_groups=mesh['hi'=16,'lo'=8] {'hi'}, use_global_device_ids=true, to_apply=%region_0.1 | all-reduce | flops 1024 | bytes 8192 | tf_op jit(solution)/shard_map/psum | solution.py:116
  182.0 35.1 %psum.15 = f32[32,32]{0,1:T(8,128)S(1)} all-reduce(f32[32,32]{0,1:T(8,128)S(1)} %psum.14), channel_id=1, replica_groups=mesh['hi'=16,'lo'=8] {'lo'}, use_global_device_ids=true, to_apply=%region_1.2 | all-reduce | flops 1024 | bytes 8192 | tf_op jit(solution)/shard_map/psum | solution.py:116
  217.1 0.1 copy.35
  217.2 2.9 %cholesky.17 = f32[32,32]{1,0:T(8,128)S(1)} custom-call(f32[32,32]{1,0:T(8,128)S(1)} %fusion.138), custom_call_target="Cholesky" | custom-call | tf_op jit(solution)/shard_map/jit(cholesky)/cholesky | solution.py:117
  220.1 0.6 compare_reduce_fusion
  220.8 0.7 fusion.139
  221.4 2.4 %custom-call.7 = f32[1,32,32]{1,2,0:T(8,128)S(1)} custom-call(f32[1,32,32]{2,1,0:T(8,128)S(1)} %get-tuple-element.11), custom_call_target="InvertDiagBlocksLowerTriangular" | custom-call | tf_op jit(solution)/shard_map/jit(_solve_triangular)/triangular_solve | solution.py:118
  223.8 0.2 fusion.136
  224.1 3.2 %fusion.154 = f32[32,16384]{1,0:T(8,128)} fusion(f32[32,32]{1,0:T(8,128)S(1)} %fusion.136, f32[32,16384]{1,0:T(8,128)S(1)} %fusion.2), kind=kOutput, calls=%fused_computation.175 | convolution fusion | flops 201326592 | bytes 4198400 | tf_op jit(solution)/shard_map/dot_general | solution.py:121
  227.3 0.7 copy.36
  (20 shorter events, 0.1 us)
Async XLA Ops:
  3.8 11.5 %copy-start = (s32[20]{0:T(128)S(1)}, s32[20]{0:T(128)}, u32[]{:S(2)}) copy-start(s32[20]{0:T(128)} %param.7) | copy-start | bytes 244
  3.8 16.8 %copy-start.1 = (s32[21]{0:T(128)S(1)}, s32[21]{0:T(128)}, u32[]{:S(2)}) copy-start(s32[21]{0:T(128)} %param.6) | copy-start | bytes 256
  3.8 41.6 %all-to-all-start = ((f32[32,128,128]{2,0,1:T(8,128)}), f32[32,128,128]{2,0,1:T(8,128)S(1)}, u32[]{:S(2)}, u32[]{:S(2)}) async-start(f32[32,128,128]{2,0,1:T(8,128)} %copy_bitcast_fusion), calls=%async_computation | async-start | bytes 4194304 | tf_op jit(solution)/shard_map/all_to_all | solution.py:98
  55.5 54.7 %all-to-all-start.1 = ((f32[32,128,128]{2,0,1:T(8,128)}), f32[32,128,128]{2,0,1:T(8,128)}, u32[]{:S(2)}, u32[]{:S(2)}) async-start(f32[32,128,128]{2,0,1:T(8,128)} %copy.32), calls=%async_computation.1 | async-start | bytes 4194304 | tf_op jit(solution)/shard_map/all_to_all | solution.py:109
